TPU v7x, 512 devices: a whole 4x8x8 slice. The times are simulated.
512 devices in a mesh: group: 8 (over y), mesh: 32 (over z, x), comp: 2 (over core).
Axes of the slice: x: 4, y: 8, z: 8, core: 2. Of those that a mesh axis runs over, the one named last changes fastest.
Arguments:
- log_sigma: float32 [2048, 128], P('mesh'), may hold values from -1 to 1
- block_owner: int32 [8, 4096, 1], P('group', 'mesh'), may hold values from 0 to 31; in each aligned block of 128 rows (0 to 127, 128 to 255, ..., all dimensions but the last counted through in order) at most 8 rows name the same one
- block_slot: int32 [8, 4096], P('group', 'mesh'), may hold values from 0 to 63
- coupling: float32 [128, 128], replicated, may hold values from -0.6 to 10, as said below
- sources: float32 [8, 2, 8, 4096, 128], P('group', 'comp', None, 'mesh'), may hold values from -24 to 24
- rcv_cell: int32 [8, 4096], P('group', 'mesh'), may hold values from 0 to 16383
- observed: float32 [8, 2, 8, 4096], P('group', 'comp', None, 'mesh'), may hold values from -6 to 6
Outputs:
- gradient: float32 [2048, 128], P('mesh')
Inputs may be any that keep to these rules, and one draw needn't show every extreme that they name: `block_owner`: in the 128 rows of one device of a group, no owner is named more than 8 times; some owner is named exactly 8 times in some device's rows. `rcv_cell`: A receiver's cell counts from the first cell of the modelling section of the device that holds the receiver's entry. `coupling`: every diagonal entry is 6 or more.
All inputs are finite; a program needn't handle non-finite values.
Results may differ from a plain program's by a relative error of at most 0.0003.
Values sent between devices are 32-bit elements; how exact they have to be, the bound alone decides.
A program may use at most 64 MiB of HBM per device.

v0:
```python
import jax
import jax.numpy as jnp
from jax import lax
from jax.sharding import PartitionSpec as P

CELLS = 128
S = 8
ITERS = 6
omega_freq = 0.8
chain_weight = 1.0


def from_partner(value, axis, distance):
    mask = 2**distance
    pairs = [(source, source ^ mask) for source in range(lax.axis_size(axis))]
    return lax.ppermute(value, axis, pairs)


def with_halo(x, sides, width):
    for axis, dim in sides:
        size, length = (lax.axis_size(axis), x.shape[dim])
        up = [(i, (i + 1) % size) for i in range(size - 1)]
        down = [(j, i) for i, j in up]
        last = lax.slice_in_dim(x, length - width, length, axis=dim)
        initial = lax.slice_in_dim(x, 0, width, axis=dim)
        before = lax.ppermute(last, axis, up)
        after = lax.ppermute(initial, axis, down)
        x = jnp.concatenate([before, x, after], axis=dim)
    return x


def partner(values):
    return from_partner(values, "comp", 0)


def beside(values):
    padded = with_halo(values, (("mesh", 1),), 1)
    return padded[:, :-2] + padded[:, 2:]


def cell_product(values, matrix):
    shaped = values.reshape(values.shape[:-1] + (-1, CELLS))
    product = jnp.einsum("...bj,ij->...bi", shaped, matrix, precision=lax.Precision.HIGHEST)
    return product.reshape(values.shape)


def operate(values, matrix, cross_coef):
    return (
        cell_product(values, matrix) - chain_weight * beside(values) + cross_coef * partner(values)
    )


def relax(right, matrix, cross_coef, inverse_diag, apply_op):
    state = jnp.zeros_like(right)
    for iteration in range(ITERS):
        state = state + inverse_diag * (right - apply_op(state, matrix, cross_coef))
    return state


def local(log_sigma, block_owner, block_slot, coupling, sources, rcv_cell, observed):
    owners = block_owner[0, :, 0]
    slots = block_slot[0]
    blocks_dev = owners.shape[0]
    inv_rows = log_sigma.shape[0]
    targets = owners * inv_rows + slots
    gathered = lax.all_gather(log_sigma, "mesh", axis=0, tiled=True)
    model_part = jnp.take(gathered, targets, axis=0)
    sigmas = jnp.exp(model_part).reshape(-1)
    receivers = rcv_cell[0]
    parity = (2 * lax.axis_index("comp") - 1).astype(jnp.float32)
    forward_coef = parity * omega_freq * sigmas
    inverse_diag = jnp.tile(1.0 / jnp.diagonal(coupling), blocks_dev)
    right = sources.reshape(S, -1)
    field_now = relax(right, coupling, forward_coef, inverse_diag, operate)
    field_other = partner(field_now)
    misfit = field_now[:, receivers] - observed[0, 0]
    adjoint_src = jnp.zeros_like(right).at[:, receivers].add(misfit)
    adjoint = relax(adjoint_src, coupling.T, -forward_coef, inverse_diag, operate)
    weighted = -parity * jnp.sum(adjoint * field_other, axis=0)
    partial_rows = (omega_freq * sigmas * weighted).reshape(blocks_dev, CELLS)
    inside_rows = (targets >= 0) & (targets < inv_rows * lax.axis_size("mesh"))
    kept_rows = jnp.where(inside_rows, targets, inv_rows * lax.axis_size("mesh"))
    owned = lax.psum_scatter(
        jnp.zeros((inv_rows * lax.axis_size("mesh"), CELLS), jnp.float32)
        .at[kept_rows]
        .add(partial_rows, mode="drop"),
        "mesh",
        scatter_dimension=0,
        tiled=True,
    )
    return lax.psum(owned, ("group", "comp"))


def solution(mesh):
    in_specs = (
        P("mesh", None),
        P("group", "mesh", None),
        P("group", "mesh"),
        P(),
        P("group", "comp", None, "mesh", None),
        P("group", "mesh"),
        P("group", "comp", None, "mesh"),
    )
    out_specs = P("mesh", None)
    return jax.shard_map(local, mesh=mesh, in_specs=in_specs, out_specs=out_specs, check_vma=False)
```

profile of v0, /device:TPU:32, one launch (start us, length us, event | category | flops | bytes accessed | tf_op | source)
XLA Modules:
  0.0 532.8 jit_solution(2460921501740615536)
XLA Ops:
  8.6 4.5 collective-permute-start
  18.4 78.7 %all-gather.2.cloned.1.call-done = f32[2048,128]{1,0:T(8,128)} async-done(((f32[64,128]{1,0:T(8,128)}), f32[2048,128]{1,0:T(8,128)}) %all-gather.2.cloned.1.call-update) | async-done | bytes 1048592 | tf_op jit(solution)/shard_map/all_gather | solution.py:66
  104.1 4.5 collective-permute-start.3
  109.9 1.9 fusion.10
  115.2 4.8 collective-permute-start.6
  125.1 4.8 collective-permute-start.9
  135.4 4.8 collective-permute-start.12
  142.1 1.9 collective-permute-start.17
  146.1 5.5 %collective-permute-start.15 = (f32[8,1]{1,0:T(8,128)S(1)}, f32[8,1]{1,0:T(8,128)S(1)}, u32[]{:S(2)}, u32[]{:S(2)}) collective-permute-start(f32[8,1]{1,0:T(8,128)S(1)} %get-tuple-element.17), channel_id=1, source_target_pairs={{0,2},{2,4},{4,6},{6,8},{8,10},{10,12},{12,14},{14,16},{16,18},{18... | collective-permute-start | bytes 104 | tf_op jit(solution)/shard_map/ppermute | solution.py:26
  154.8 5.3 copy.271
  160.1 6.0 %scatter_custom_fusion = f32[8,16384]{0,1:T(8,128)} fusion(s32[128]{0:T(128)S(1)} %fusion.122, f32[]{:T(128)} %constant.12.clone.1, f32[1,1,8,128]{2,3,1,0:T(8,128)S(1)} %copy.272, f32[8,16384]{0,1:T(8,128)} %copy.271, s32[1024]{0:T(1024)S(1)} %pad_clamp_fusion), kind=kCustom, calls=%fused_computation.15 | custom fusion | flops 2048 | bytes 1118212 | tf_op jit(solution)/shard_map/scatter-add | solution.py:77
  166.1 5.5 %copy.273 = f32[8,16384]{1,0:T(8,128)S(1)} copy(f32[8,16384]{0,1:T(8,128)} %scatter_custom_fusion) | data formatting | bytes 1048576 | tf_op jit(solution)/shard_map/scatter-add | solution.py:77
  175.3 6.9 %collective-permute-start.18 = (f32[8,1]{1,0:T(8,128)S(1)}, f32[8,1]{1,0:T(8,128)S(1)}, u32[]{:S(2)}, u32[]{:S(2)}) collective-permute-start(f32[8,1]{1,0:T(8,128)S(1)} %get-tuple-element.15), channel_id=1, source_target_pairs={{0,2},{2,4},{4,6},{6,8},{8,10},{10,12},{12,14},{14,16},{16,18},{18... | collective-permute-start | bytes 104 | tf_op jit(solution)/shard_map/ppermute | solution.py:26
  184.2 1.9 collective-permute-start.23
  187.5 6.9 %collective-permute-start.21 = (f32[8,1]{1,0:T(8,128)S(1)}, f32[8,1]{1,0:T(8,128)S(1)}, u32[]{:S(2)}, u32[]{:S(2)}) collective-permute-start(f32[8,1]{1,0:T(8,128)S(1)} %get-tuple-element.13), channel_id=1, source_target_pairs={{0,2},{2,4},{4,6},{6,8},{8,10},{10,12},{12,14},{14,16},{16,18},{18... | collective-permute-start | bytes 104 | tf_op jit(solution)/shard_map/ppermute | solution.py:26
  199.5 6.9 %collective-permute-start.24 = (f32[8,1]{1,0:T(8,128)S(1)}, f32[8,1]{1,0:T(8,128)S(1)}, u32[]{:S(2)}, u32[]{:S(2)}) collective-permute-start(f32[8,1]{1,0:T(8,128)S(1)} %get-tuple-element.11), channel_id=1, source_target_pairs={{0,2},{2,4},{4,6},{6,8},{8,10},{10,12},{12,14},{14,16},{16,18},{18... | collective-permute-start | bytes 104 | tf_op jit(solution)/shard_map/ppermute | solution.py:26
  208.4 1.9 collective-permute-start.29
  210.3 2.4 collective-permute-start.33
  214.1 6.9 %collective-permute-start.27 = (f32[8,1]{1,0:T(8,128)S(1)}, f32[8,1]{1,0:T(8,128)S(1)}, u32[]{:S(2)}, u32[]{:S(2)}) collective-permute-start(f32[8,1]{1,0:T(8,128)S(1)} %get-tuple-element.9), channel_id=1, source_target_pairs={{0,2},{2,4},{4,6},{6,8},{8,10},{10,12},{12,14},{14,16},{16,18},{18... | collective-permute-start | bytes 104 | tf_op jit(solution)/shard_map/ppermute | solution.py:26
  222.8 1.9 collective-permute-start.32
  226.1 6.9 %collective-permute-start.30 = (f32[8,1]{1,0:T(8,128)S(1)}, f32[8,1]{1,0:T(8,128)S(1)}, u32[]{:S(2)}, u32[]{:S(2)}) collective-permute-start(f32[8,1]{1,0:T(8,128)S(1)} %get-tuple-element.7), channel_id=1, source_target_pairs={{0,2},{2,4},{4,6},{6,8},{8,10},{10,12},{12,14},{14,16},{16,18},{18... | collective-permute-start | bytes 104 | tf_op jit(solution)/shard_map/ppermute | solution.py:26
  234.7 2.1 scatter_custom_fusion.1
  236.8 242.3 %reduce-scatter.2.cloned.1.call-done = f32[64,128]{1,0:T(8,128)} async-done(((f32[2048,128]{1,0:T(8,128)}), f32[64,128]{1,0:T(8,128)}) %reduce-scatter.2.cloned.1.call-update) | async-done | bytes 32784 | tf_op jit(solution)/shard_map/reduce_scatter | solution.py:83
  479.1 46.9 %psum.7 = f32[64,128]{1,0:T(8,128)} all-reduce(f32[64,128]{1,0:T(8,128)} %reduce-scatter.2.cloned.1.call-done), channel_id=1, replica_groups=mesh['group'=8,'mesh'=32,'comp'=2] {'group','comp'}, use_global_device_ids=true, to_apply=%region_4.5 | all-reduce | flops 8192 | bytes 65536 | tf_op jit(solution)/shard_map/psum | solution.py:91
  (106 shorter events, 56.4 us)
Async XLA Ops:
  6.5 90.6 %all-gather.2.cloned.1.call-start = ((), (), s32[]{:S(2)}) async-start(), calls=%async_computation.1 | async-start | bytes 1081344 | tf_op jit(solution)/shard_map/all_gather | solution.py:66
  7.3 471.8 %reduce-scatter.2.cloned.1.call-start = ((), (), s32[]{:S(2)}) async-start(), calls=%async_computation.2 | async-start | bytes 1081344 | tf_op jit(solution)/shard_map/reduce_scatter | solution.py:83
  7.3 91.8 %collective-permute-start.1 = (f32[8,1]{1,0:T(8,128)S(1)}, f32[8,1]{1,0:T(8,128)S(1)}, u32[]{:S(2)}, u32[]{:S(2)}) collective-permute-start(f32[8,1]{1,0:T(8,128)S(1)} %broadcast.157), channel_id=1, source_target_pairs={{2,0},{4,2},{6,4},{8,6},{10,8},{12,10},{14,12},{16,14},{18,16},{20... | collective-permute-start | bytes 104 | tf_op jit(solution)/shard_map/ppermute | solution.py:27
  8.6 90.5 %collective-permute-start = (f32[8,1]{1,0:T(8,128)S(1)}, f32[8,1]{1,0:T(8,128)S(1)}, u32[]{:S(2)}, u32[]{:S(2)}) collective-permute-start(f32[8,1]{1,0:T(8,128)S(1)} %broadcast.157), channel_id=1, source_target_pairs={{0,2},{2,4},{4,6},{6,8},{8,10},{10,12},{12,14},{14,16},{16,18},{18... | collective-permute-start | bytes 104 | tf_op jit(solution)/shard_map/ppermute | solution.py:26
  13.2 85.8 %collective-permute-start.2 = (f32[8,16384]{1,0:T(8,128)S(1)}, f32[8,16384]{1,0:T(8,128)S(1)}, u32[]{:S(2)}, u32[]{:S(2)}) collective-permute-start(f32[8,16384]{1,0:T(8,128)S(1)} %broadcast.154.clone), channel_id=1, source_target_pairs={{0,1},{1,0},{2,3},{3,2},{4,5},{5,4},{6,7},{7,6},{8,9},{9,8},{10,11... | collective-permute-start | bytes 1572872 | tf_op jit(solution)/shard_map/ppermute | solution.py:16
  100.8 9.2 %collective-permute-start.5 = (f32[8,16384]{1,0:T(8,128)S(1)}, f32[8,16384]{1,0:T(8,128)S(1)}, u32[]{:S(2)}, u32[]{:S(2)}) collective-permute-start(f32[8,16384]{1,0:T(8,128)S(1)} %fusion.8), channel_id=1, source_target_pairs={{0,1},{1,0},{2,3},{3,2},{4,5},{5,4},{6,7},{7,6},{8,9},{9,8},{10,11... | collective-permute-start | bytes 1572872 | tf_op jit(solution)/shard_map/ppermute | solution.py:16
  111.9 9.4 %collective-permute-start.8 = (f32[8,16384]{1,0:T(8,128)S(1)}, f32[8,16384]{1,0:T(8,128)S(1)}, u32[]{:S(2)}, u32[]{:S(2)}) collective-permute-start(f32[8,16384]{1,0:T(8,128)S(1)} %fusion.10), channel_id=1, source_target_pairs={{0,1},{1,0},{2,3},{3,2},{4,5},{5,4},{6,7},{7,6},{8,9},{9,8},{10,11... | collective-permute-start | bytes 1572872 | tf_op jit(solution)/shard_map/ppermute | solution.py:16
  121.8 9.4 %collective-permute-start.11 = (f32[8,16384]{1,0:T(8,128)S(1)}, f32[8,16384]{1,0:T(8,128)S(1)}, u32[]{:S(2)}, u32[]{:S(2)}) collective-permute-start(f32[8,16384]{1,0:T(8,128)S(1)} %fusion.12), channel_id=1, source_target_pairs={{0,1},{1,0},{2,3},{3,2},{4,5},{5,4},{6,7},{7,6},{8,9},{9,8},{10,11... | collective-permute-start | bytes 1572872 | tf_op jit(solution)/shard_map/ppermute | solution.py:16
  132.1 9.4 %collective-permute-start.14 = (f32[8,16384]{1,0:T(8,128)S(1)}, f32[8,16384]{1,0:T(8,128)S(1)}, u32[]{:S(2)}, u32[]{:S(2)}) collective-permute-start(f32[8,16384]{1,0:T(8,128)S(1)} %fusion.14), channel_id=1, source_target_pairs={{0,1},{1,0},{2,3},{3,2},{4,5},{5,4},{6,7},{7,6},{8,9},{9,8},{10,11... | collective-permute-start | bytes 1572872 | tf_op jit(solution)/shard_map/ppermute | solution.py:16
  142.1 10.8 %collective-permute-start.17 = (f32[8,16384]{1,0:T(8,128)S(1)}, f32[8,16384]{1,0:T(8,128)}, u32[]{:S(2)}, u32[]{:S(2)}) collective-permute-start(f32[8,16384]{1,0:T(8,128)S(1)} %fusion.16), channel_id=1, source_target_pairs={{0,1},{1,0},{2,3},{3,2},{4,5},{5,4},{6,7},{7,6},{8,9},{9,8},{10,11... | collective-permute-start | bytes 1572872 | tf_op jit(solution)/shard_map/ppermute | solution.py:16
  172.0 11.5 %collective-permute-start.20 = (f32[8,16384]{1,0:T(8,128)S(1)}, f32[8,16384]{1,0:T(8,128)S(1)}, u32[]{:S(2)}, u32[]{:S(2)}) collective-permute-start(f32[8,16384]{1,0:T(8,128)S(1)} %fusion.5), channel_id=1, source_target_pairs={{0,1},{1,0},{2,3},{3,2},{4,5},{5,4},{6,7},{7,6},{8,9},{9,8},{10,11... | collective-permute-start | bytes 1572872 | tf_op jit(solution)/shard_map/ppermute | solution.py:16
  174.0 8.2 %collective-permute-start.19 = (f32[8,1]{1,0:T(8,128)S(1)}, f32[8,1]{1,0:T(8,128)S(1)}, u32[]{:S(2)}, u32[]{:S(2)}) collective-permute-start(f32[8,1]{1,0:T(8,128)S(1)} %get-tuple-element.16), channel_id=1, source_target_pairs={{2,0},{4,2},{6,4},{8,6},{10,8},{12,10},{14,12},{16,14},{18,16},{20... | collective-permute-start | bytes 104 | tf_op jit(solution)/shard_map/ppermute | solution.py:27
  175.3 8.3 %collective-permute-start.18 = (f32[8,1]{1,0:T(8,128)S(1)}, f32[8,1]{1,0:T(8,128)S(1)}, u32[]{:S(2)}, u32[]{:S(2)}) collective-permute-start(f32[8,1]{1,0:T(8,128)S(1)} %get-tuple-element.15), channel_id=1, source_target_pairs={{0,2},{2,4},{4,6},{6,8},{8,10},{10,12},{12,14},{14,16},{16,18},{18... | collective-permute-start | bytes 104 | tf_op jit(solution)/shard_map/ppermute | solution.py:26
  184.2 11.5 %collective-permute-start.23 = (f32[8,16384]{1,0:T(8,128)S(1)}, f32[8,16384]{1,0:T(8,128)S(1)}, u32[]{:S(2)}, u32[]{:S(2)}) collective-permute-start(f32[8,16384]{1,0:T(8,128)S(1)} %fusion.50), channel_id=1, source_target_pairs={{0,1},{1,0},{2,3},{3,2},{4,5},{5,4},{6,7},{7,6},{8,9},{9,8},{10,11... | collective-permute-start | bytes 1572872 | tf_op jit(solution)/shard_map/ppermute | solution.py:16
  186.2 8.8 %collective-permute-start.22 = (f32[8,1]{1,0:T(8,128)S(1)}, f32[8,1]{1,0:T(8,128)S(1)}, u32[]{:S(2)}, u32[]{:S(2)}) collective-permute-start(f32[8,1]{1,0:T(8,128)S(1)} %get-tuple-element.14), channel_id=1, source_target_pairs={{2,0},{4,2},{6,4},{8,6},{10,8},{12,10},{14,12},{16,14},{18,16},{20... | collective-permute-start | bytes 104 | tf_op jit(solution)/shard_map/ppermute | solution.py:27
  187.5 8.2 %collective-permute-start.21 = (f32[8,1]{1,0:T(8,128)S(1)}, f32[8,1]{1,0:T(8,128)S(1)}, u32[]{:S(2)}, u32[]{:S(2)}) collective-permute-start(f32[8,1]{1,0:T(8,128)S(1)} %get-tuple-element.13), channel_id=1, source_target_pairs={{0,2},{2,4},{4,6},{6,8},{8,10},{10,12},{12,14},{14,16},{16,18},{18... | collective-permute-start | bytes 104 | tf_op jit(solution)/shard_map/ppermute | solution.py:26
  196.2 11.5 %collective-permute-start.26 = (f32[8,16384]{1,0:T(8,128)S(1)}, f32[8,16384]{1,0:T(8,128)S(1)}, u32[]{:S(2)}, u32[]{:S(2)}) collective-permute-start(f32[8,16384]{1,0:T(8,128)S(1)} %fusion.44), channel_id=1, source_target_pairs={{0,1},{1,0},{2,3},{3,2},{4,5},{5,4},{6,7},{7,6},{8,9},{9,8},{10,11... | collective-permute-start | bytes 1572872 | tf_op jit(solution)/shard_map/ppermute | solution.py:16
  208.4 14.0 %collective-permute-start.29 = (f32[8,16384]{1,0:T(8,128)S(1)}, f32[8,16384]{1,0:T(8,128)S(1)}, u32[]{:S(2)}, u32[]{:S(2)}) collective-permute-start(f32[8,16384]{1,0:T(8,128)S(1)} %fusion.38), channel_id=1, source_target_pairs={{0,1},{1,0},{2,3},{3,2},{4,5},{5,4},{6,7},{7,6},{8,9},{9,8},{10,11... | collective-permute-start | bytes 1572872 | tf_op jit(solution)/shard_map/ppermute | solution.py:16
  210.3 23.2 %collective-permute-start.33 = (f32[8,16384]{1,0:T(8,128)S(1)}, f32[8,16384]{1,0:T(8,128)S(1)}, u32[]{:S(2)}, u32[]{:S(2)}) collective-permute-start(f32[8,16384]{1,0:T(8,128)S(1)} %fusion.18), channel_id=1, source_target_pairs={{0,1},{1,0},{2,3},{3,2},{4,5},{5,4},{6,7},{7,6},{8,9},{9,8},{10,11... | collective-permute-start | bytes 1572872 | tf_op jit(solution)/shard_map/ppermute | solution.py:16
  212.8 8.8 %collective-permute-start.28 = (f32[8,1]{1,0:T(8,128)S(1)}, f32[8,1]{1,0:T(8,128)S(1)}, u32[]{:S(2)}, u32[]{:S(2)}) collective-permute-start(f32[8,1]{1,0:T(8,128)S(1)} %get-tuple-element.10), channel_id=1, source_target_pairs={{2,0},{4,2},{6,4},{8,6},{10,8},{12,10},{14,12},{16,14},{18,16},{20... | collective-permute-start | bytes 104 | tf_op jit(solution)/shard_map/ppermute | solution.py:27
  214.1 8.3 %collective-permute-start.27 = (f32[8,1]{1,0:T(8,128)S(1)}, f32[8,1]{1,0:T(8,128)S(1)}, u32[]{:S(2)}, u32[]{:S(2)}) collective-permute-start(f32[8,1]{1,0:T(8,128)S(1)} %get-tuple-element.9), channel_id=1, source_target_pairs={{0,2},{2,4},{4,6},{6,8},{8,10},{10,12},{12,14},{14,16},{16,18},{18... | collective-permute-start | bytes 104 | tf_op jit(solution)/shard_map/ppermute | solution.py:26
  222.8 11.5 %collective-permute-start.32 = (f32[8,16384]{1,0:T(8,128)S(1)}, f32[8,16384]{1,0:T(8,128)S(1)}, u32[]{:S(2)}, u32[]{:S(2)}) collective-permute-start(f32[8,16384]{1,0:T(8,128)S(1)} %fusion.32), channel_id=1, source_target_pairs={{0,1},{1,0},{2,3},{3,2},{4,5},{5,4},{6,7},{7,6},{8,9},{9,8},{10,11... | collective-permute-start | bytes 1572872 | tf_op jit(solution)/shard_map/ppermute | solution.py:16
  224.8 8.8 %collective-permute-start.31 = (f32[8,1]{1,0:T(8,128)S(1)}, f32[8,1]{1,0:T(8,128)S(1)}, u32[]{:S(2)}, u32[]{:S(2)}) collective-permute-start(f32[8,1]{1,0:T(8,128)S(1)} %get-tuple-element.8), channel_id=1, source_target_pairs={{2,0},{4,2},{6,4},{8,6},{10,8},{12,10},{14,12},{16,14},{18,16},{20... | collective-permute-start | bytes 104 | tf_op jit(solution)/shard_map/ppermute | solution.py:27
  226.1 8.2 %collective-permute-start.30 = (f32[8,1]{1,0:T(8,128)S(1)}, f32[8,1]{1,0:T(8,128)S(1)}, u32[]{:S(2)}, u32[]{:S(2)}) collective-permute-start(f32[8,1]{1,0:T(8,128)S(1)} %get-tuple-element.7), channel_id=1, source_target_pairs={{0,2},{2,4},{4,6},{6,8},{8,10},{10,12},{12,14},{14,16},{16,18},{18... | collective-permute-start | bytes 104 | tf_op jit(solution)/shard_map/ppermute | solution.py:26
  (16 other events, 464.6 us)
Sparse Core Ops, SparseCore 0:
  10.5 86.5 all-gather.1
  237.0 242.0 reduce-scatter.1
where the time goes:
time: 534 us; the launch traced here: 533 us
  waiting for transfers between devices  332 us (62%)
  starting transfers between devices  101 us (19%)
  blocking collectives  46.9 us (9%)
  local copies, waits for them, and re-layouts  14.9 us (3%)
  between operations  14 us (3%)
  other arithmetic  13.9 us (3%)
  matrix products  10.1 us (2%)
    reduce_scatter x1, waiting for transfers between devices, local(): lax.psum_scatter(jnp.zeros((inv_rows * lax.axis_size('mesh'), CELLS), jnp...  242 us
    all_gather x1, waiting for transfers between devices, local(): gathered = lax.all_gather(log_sigma, 'mesh', axis=0, tiled=True)  78.7 us
    ppermute x11, starting transfers between devices, with_halo(): before = lax.ppermute(last, axis, up)  63.6 us
    psum x1, blocking collectives, local(): return lax.psum(owned, ('group', 'comp'))  46.9 us
    ppermute x12, starting transfers between devices, from_partner(): return lax.ppermute(value, axis, pairs)  23.5 us
    ppermute x11, starting transfers between devices, with_halo(): after = lax.ppermute(initial, axis, down)  14.1 us
  transfers between devices with their start and end apart: 36, of which 12 were waited for; matrix products, arithmetic and copies ran while one was open for 2% of the time, Pallas kernels for 0%

commit v1 on v0

--- a/solution.py
+++ b/solution.py
@@ -1,3 +1,4 @@
+import functools
 import jax
 import jax.numpy as jnp
 from jax import lax
@@ -8,6 +9,15 @@
 ITERS = 6
 omega_freq = 0.8
 chain_weight = 1.0
+
+
+def show_loads(chunk, row_axis, link_axis):
+    for it in (row_axis, link_axis):
+        chunk = jax.lax.psum(chunk, it)
+    return chunk
+
+
+treat_slabs_for = functools.partial(show_loads, row_axis="group", link_axis="comp")
 
 
 def from_partner(value, axis, distance):
@@ -88,7 +98,7 @@
         scatter_dimension=0,
         tiled=True,
     )
-    return lax.psum(owned, ("group", "comp"))
+    return treat_slabs_for(owned)
 
 
 def solution(mesh):

time: 534 us -> 523 us (0.979)
  the two profiles are of different devices: /device:TPU:32 before, /device:TPU:1 now
where the time goes in v1:
time: 523 us; the launch traced here: 522 us
  waiting for transfers between devices  311 us (59%)
  starting transfers between devices  118 us (23%)
  blocking collectives  40.1 us (8%)
  local copies, waits for them, and re-layouts  14.8 us (3%)
  between operations  14 us (3%)
  other arithmetic  13.8 us (3%)
  matrix products  10.1 us (2%)
    reduce_scatter x1, waiting for transfers between devices, local(): lax.psum_scatter(jnp.zeros((inv_rows * lax.axis_size('mesh'), CELLS), jnp...  237 us
    all_gather x1, waiting for transfers between devices, local(): gathered = lax.all_gather(log_sigma, 'mesh', axis=0, tiled=True)  68.6 us
    ppermute x11, starting transfers between devices, with_halo(): before = lax.ppermute(last, axis, up)  60.5 us
    ppermute x12, starting transfers between devices, from_partner(): return lax.ppermute(value, axis, pairs)  43.4 us
    psum x2, blocking collectives, show_loads(): chunk = jax.lax.psum(chunk, it)  40.1 us
    ppermute x11, starting transfers between devices, with_halo(): after = lax.ppermute(initial, axis, down)  14.1 us
  transfers between devices with their start and end apart: 36, of which 12 were waited for; matrix products, arithmetic and copies ran while one was open for 2% of the time, Pallas kernels for 0%

profile of v1, /device:TPU:1, one launch (start us, length us, event | category | flops | bytes accessed | tf_op | source)
XLA Modules:
  0.0 522.0 jit_solution(16118567560543336165)
XLA Ops:
  8.6 4.6 collective-permute-start
  13.3 8.8 %collective-permute-start.2 = (f32[8,16384]{1,0:T(8,128)S(1)}, f32[8,16384]{1,0:T(8,128)S(1)}, u32[]{:S(2)}, u32[]{:S(2)}) collective-permute-start(f32[8,16384]{1,0:T(8,128)S(1)} %broadcast.154.clone), channel_id=1, source_target_pairs={{0,1},{1,0},{2,3},{3,2},{4,5},{5,4},{6,7},{7,6},{8,9},{9,8},{10,11... | collective-permute-start | bytes 1572872 | tf_op jit(solution)/shard_map/ppermute | solution.py:26
  25.3 68.6 %all-gather.2.cloned.1.call-done = f32[2048,128]{1,0:T(8,128)} async-done(((f32[64,128]{1,0:T(8,128)}), f32[2048,128]{1,0:T(8,128)}) %all-gather.2.cloned.1.call-update) | async-done | bytes 1048592 | tf_op jit(solution)/shard_map/all_gather | solution.py:76
  97.5 7.0 %collective-permute-start.5 = (f32[8,16384]{1,0:T(8,128)S(1)}, f32[8,16384]{1,0:T(8,128)S(1)}, u32[]{:S(2)}, u32[]{:S(2)}) collective-permute-start(f32[8,16384]{1,0:T(8,128)S(1)} %fusion.8), channel_id=1, source_target_pairs={{0,1},{1,0},{2,3},{3,2},{4,5},{5,4},{6,7},{7,6},{8,9},{9,8},{10,11... | collective-permute-start | bytes 1572872 | tf_op jit(solution)/shard_map/ppermute | solution.py:26
  105.9 4.0 collective-permute-start.3
  112.6 3.1 collective-permute-start.8
  117.0 4.5 collective-permute-start.6
  126.9 4.5 collective-permute-start.9
  133.1 2.8 collective-permute-start.14
  137.3 4.5 collective-permute-start.12
  147.9 5.2 collective-permute-start.15
  155.8 5.3 %copy.271 = f32[8,16384]{0,1:T(8,128)} copy(f32[8,16384]{1,0:T(8,128)S(1)} %fusion.18) | data formatting | bytes 1048576 | tf_op jit(solution)/shard_map/add | solution.py:66
  161.1 6.0 %scatter_custom_fusion = f32[8,16384]{0,1:T(8,128)} fusion(s32[128]{0:T(128)S(1)} %fusion.122, f32[]{:T(128)} %constant.12.clone.1, f32[1,1,8,128]{2,3,1,0:T(8,128)S(1)} %copy.272, f32[8,16384]{0,1:T(8,128)} %copy.271, s32[1024]{0:T(1024)S(1)} %pad_clamp_fusion), kind=kCustom, calls=%fused_computation.15 | custom fusion | flops 2048 | bytes 1118212 | tf_op jit(solution)/shard_map/scatter-add | solution.py:87
  167.0 5.5 %copy.273 = f32[8,16384]{1,0:T(8,128)S(1)} copy(f32[8,16384]{0,1:T(8,128)} %scatter_custom_fusion) | data formatting | bytes 1048576 | tf_op jit(solution)/shard_map/scatter-add | solution.py:87
  177.2 6.6 %collective-permute-start.18 = (f32[8,1]{1,0:T(8,128)S(1)}, f32[8,1]{1,0:T(8,128)S(1)}, u32[]{:S(2)}, u32[]{:S(2)}) collective-permute-start(f32[8,1]{1,0:T(8,128)S(1)} %get-tuple-element.15), channel_id=1, source_target_pairs={{0,2},{2,4},{4,6},{6,8},{8,10},{10,12},{12,14},{14,16},{16,18},{18... | collective-permute-start | bytes 104 | tf_op jit(solution)/shard_map/ppermute | solution.py:36
  189.4 6.6 %collective-permute-start.21 = (f32[8,1]{1,0:T(8,128)S(1)}, f32[8,1]{1,0:T(8,128)S(1)}, u32[]{:S(2)}, u32[]{:S(2)}) collective-permute-start(f32[8,1]{1,0:T(8,128)S(1)} %get-tuple-element.13), channel_id=1, source_target_pairs={{0,2},{2,4},{4,6},{6,8},{8,10},{10,12},{12,14},{14,16},{16,18},{18... | collective-permute-start | bytes 104 | tf_op jit(solution)/shard_map/ppermute | solution.py:36
  201.3 6.7 %collective-permute-start.24 = (f32[8,1]{1,0:T(8,128)S(1)}, f32[8,1]{1,0:T(8,128)S(1)}, u32[]{:S(2)}, u32[]{:S(2)}) collective-permute-start(f32[8,1]{1,0:T(8,128)S(1)} %get-tuple-element.11), channel_id=1, source_target_pairs={{0,2},{2,4},{4,6},{6,8},{8,10},{10,12},{12,14},{14,16},{16,18},{18... | collective-permute-start | bytes 104 | tf_op jit(solution)/shard_map/ppermute | solution.py:36
  209.4 2.8 collective-permute-start.29
  215.5 6.6 %collective-permute-start.27 = (f32[8,1]{1,0:T(8,128)S(1)}, f32[8,1]{1,0:T(8,128)S(1)}, u32[]{:S(2)}, u32[]{:S(2)}) collective-permute-start(f32[8,1]{1,0:T(8,128)S(1)} %get-tuple-element.9), channel_id=1, source_target_pairs={{0,2},{2,4},{4,6},{6,8},{8,10},{10,12},{12,14},{14,16},{16,18},{18... | collective-permute-start | bytes 104 | tf_op jit(solution)/shard_map/ppermute | solution.py:36
  223.3 3.3 collective-permute-start.32
  227.9 6.6 %collective-permute-start.30 = (f32[8,1]{1,0:T(8,128)S(1)}, f32[8,1]{1,0:T(8,128)S(1)}, u32[]{:S(2)}, u32[]{:S(2)}) collective-permute-start(f32[8,1]{1,0:T(8,128)S(1)} %get-tuple-element.7), channel_id=1, source_target_pairs={{0,2},{2,4},{4,6},{6,8},{8,10},{10,12},{12,14},{14,16},{16,18},{18... | collective-permute-start | bytes 104 | tf_op jit(solution)/shard_map/ppermute | solution.py:36
  237.8 237.3 %reduce-scatter.2.cloned.1.call-done = f32[64,128]{1,0:T(8,128)} async-done(((f32[2048,128]{1,0:T(8,128)}), f32[64,128]{1,0:T(8,128)}) %reduce-scatter.2.cloned.1.call-update) | async-done | bytes 32784 | tf_op jit(solution)/shard_map/reduce_scatter | solution.py:93
  475.1 23.2 %psum.14 = f32[64,128]{1,0:T(8,128)S(1)} all-reduce(f32[64,128]{1,0:T(8,128)} %reduce-scatter.2.cloned.1.call-done), channel_id=1, replica_groups=mesh['group'=8,'mesh'=32,'comp'=2] {'group'}, use_global_device_ids=true, to_apply=%region_4.5 | all-reduce | flops 8192 | bytes 65536 | tf_op jit(solution)/shard_map/psum | solution.py:16
  498.2 16.9 %psum.15 = f32[64,128]{1,0:T(8,128)} all-reduce(f32[64,128]{1,0:T(8,128)S(1)} %psum.14), channel_id=1, replica_groups=mesh['group'=8,'mesh'=32,'comp'=2] {'comp'}, use_global_device_ids=true, to_apply=%region_5.6 | all-reduce | flops 8192 | bytes 65536 | tf_op jit(solution)/shard_map/psum | solution.py:16
  (107 shorter events, 57.0 us)
Async XLA Ops:
  6.5 87.3 %all-gather.2.cloned.1.call-start = ((), (), s32[]{:S(2)}) async-start(), calls=%async_computation.1 | async-start | bytes 1081344 | tf_op jit(solution)/shard_map/all_gather | solution.py:76
  7.3 467.8 %reduce-scatter.2.cloned.1.call-start = ((), (), s32[]{:S(2)}) async-start(), calls=%async_computation.2 | async-start | bytes 1081344 | tf_op jit(solution)/shard_map/reduce_scatter | solution.py:93
  7.3 88.5 %collective-permute-start.1 = (f32[8,1]{1,0:T(8,128)S(1)}, f32[8,1]{1,0:T(8,128)S(1)}, u32[]{:S(2)}, u32[]{:S(2)}) collective-permute-start(f32[8,1]{1,0:T(8,128)S(1)} %broadcast.157), channel_id=1, source_target_pairs={{2,0},{4,2},{6,4},{8,6},{10,8},{12,10},{14,12},{16,14},{18,16},{20... | collective-permute-start | bytes 104 | tf_op jit(solution)/shard_map/ppermute | solution.py:37
  8.6 87.2 %collective-permute-start = (f32[8,1]{1,0:T(8,128)S(1)}, f32[8,1]{1,0:T(8,128)S(1)}, u32[]{:S(2)}, u32[]{:S(2)}) collective-permute-start(f32[8,1]{1,0:T(8,128)S(1)} %broadcast.157), channel_id=1, source_target_pairs={{0,2},{2,4},{4,6},{6,8},{8,10},{10,12},{12,14},{14,16},{16,18},{18... | collective-permute-start | bytes 104 | tf_op jit(solution)/shard_map/ppermute | solution.py:36
  13.3 82.6 %collective-permute-start.2 = (f32[8,16384]{1,0:T(8,128)S(1)}, f32[8,16384]{1,0:T(8,128)S(1)}, u32[]{:S(2)}, u32[]{:S(2)}) collective-permute-start(f32[8,16384]{1,0:T(8,128)S(1)} %broadcast.154.clone), channel_id=1, source_target_pairs={{0,1},{1,0},{2,3},{3,2},{4,5},{5,4},{6,7},{7,6},{8,9},{9,8},{10,11... | collective-permute-start | bytes 1572872 | tf_op jit(solution)/shard_map/ppermute | solution.py:26
  97.5 13.1 %collective-permute-start.5 = (f32[8,16384]{1,0:T(8,128)S(1)}, f32[8,16384]{1,0:T(8,128)S(1)}, u32[]{:S(2)}, u32[]{:S(2)}) collective-permute-start(f32[8,16384]{1,0:T(8,128)S(1)} %fusion.8), channel_id=1, source_target_pairs={{0,1},{1,0},{2,3},{3,2},{4,5},{5,4},{6,7},{7,6},{8,9},{9,8},{10,11... | collective-permute-start | bytes 1572872 | tf_op jit(solution)/shard_map/ppermute | solution.py:26
  112.6 9.7 %collective-permute-start.8 = (f32[8,16384]{1,0:T(8,128)S(1)}, f32[8,16384]{1,0:T(8,128)S(1)}, u32[]{:S(2)}, u32[]{:S(2)}) collective-permute-start(f32[8,16384]{1,0:T(8,128)S(1)} %fusion.10), channel_id=1, source_target_pairs={{0,1},{1,0},{2,3},{3,2},{4,5},{5,4},{6,7},{7,6},{8,9},{9,8},{10,11... | collective-permute-start | bytes 1572872 | tf_op jit(solution)/shard_map/ppermute | solution.py:26
  122.8 9.4 %collective-permute-start.11 = (f32[8,16384]{1,0:T(8,128)S(1)}, f32[8,16384]{1,0:T(8,128)S(1)}, u32[]{:S(2)}, u32[]{:S(2)}) collective-permute-start(f32[8,16384]{1,0:T(8,128)S(1)} %fusion.12), channel_id=1, source_target_pairs={{0,1},{1,0},{2,3},{3,2},{4,5},{5,4},{6,7},{7,6},{8,9},{9,8},{10,11... | collective-permute-start | bytes 1572872 | tf_op jit(solution)/shard_map/ppermute | solution.py:26
  133.1 9.4 %collective-permute-start.14 = (f32[8,16384]{1,0:T(8,128)S(1)}, f32[8,16384]{1,0:T(8,128)S(1)}, u32[]{:S(2)}, u32[]{:S(2)}) collective-permute-start(f32[8,16384]{1,0:T(8,128)S(1)} %fusion.14), channel_id=1, source_target_pairs={{0,1},{1,0},{2,3},{3,2},{4,5},{5,4},{6,7},{7,6},{8,9},{9,8},{10,11... | collective-permute-start | bytes 1572872 | tf_op jit(solution)/shard_map/ppermute | solution.py:26
  143.1 10.8 %collective-permute-start.17 = (f32[8,16384]{1,0:T(8,128)S(1)}, f32[8,16384]{1,0:T(8,128)}, u32[]{:S(2)}, u32[]{:S(2)}) collective-permute-start(f32[8,16384]{1,0:T(8,128)S(1)} %fusion.16), channel_id=1, source_target_pairs={{0,1},{1,0},{2,3},{3,2},{4,5},{5,4},{6,7},{7,6},{8,9},{9,8},{10,11... | collective-permute-start | bytes 1572872 | tf_op jit(solution)/shard_map/ppermute | solution.py:26
  173.0 11.5 %collective-permute-start.20 = (f32[8,16384]{1,0:T(8,128)S(1)}, f32[8,16384]{1,0:T(8,128)S(1)}, u32[]{:S(2)}, u32[]{:S(2)}) collective-permute-start(f32[8,16384]{1,0:T(8,128)S(1)} %fusion.5), channel_id=1, source_target_pairs={{0,1},{1,0},{2,3},{3,2},{4,5},{5,4},{6,7},{7,6},{8,9},{9,8},{10,11... | collective-permute-start | bytes 1572872 | tf_op jit(solution)/shard_map/ppermute | solution.py:26
  175.9 7.9 %collective-permute-start.19 = (f32[8,1]{1,0:T(8,128)S(1)}, f32[8,1]{1,0:T(8,128)S(1)}, u32[]{:S(2)}, u32[]{:S(2)}) collective-permute-start(f32[8,1]{1,0:T(8,128)S(1)} %get-tuple-element.16), channel_id=1, source_target_pairs={{2,0},{4,2},{6,4},{8,6},{10,8},{12,10},{14,12},{16,14},{18,16},{20... | collective-permute-start | bytes 104 | tf_op jit(solution)/shard_map/ppermute | solution.py:37
  185.2 11.5 %collective-permute-start.23 = (f32[8,16384]{1,0:T(8,128)S(1)}, f32[8,16384]{1,0:T(8,128)S(1)}, u32[]{:S(2)}, u32[]{:S(2)}) collective-permute-start(f32[8,16384]{1,0:T(8,128)S(1)} %fusion.50), channel_id=1, source_target_pairs={{0,1},{1,0},{2,3},{3,2},{4,5},{5,4},{6,7},{7,6},{8,9},{9,8},{10,11... | collective-permute-start | bytes 1572872 | tf_op jit(solution)/shard_map/ppermute | solution.py:26
  188.1 8.5 %collective-permute-start.22 = (f32[8,1]{1,0:T(8,128)S(1)}, f32[8,1]{1,0:T(8,128)S(1)}, u32[]{:S(2)}, u32[]{:S(2)}) collective-permute-start(f32[8,1]{1,0:T(8,128)S(1)} %get-tuple-element.14), channel_id=1, source_target_pairs={{2,0},{4,2},{6,4},{8,6},{10,8},{12,10},{14,12},{16,14},{18,16},{20... | collective-permute-start | bytes 104 | tf_op jit(solution)/shard_map/ppermute | solution.py:37
  189.4 7.4 %collective-permute-start.21 = (f32[8,1]{1,0:T(8,128)S(1)}, f32[8,1]{1,0:T(8,128)S(1)}, u32[]{:S(2)}, u32[]{:S(2)}) collective-permute-start(f32[8,1]{1,0:T(8,128)S(1)} %get-tuple-element.13), channel_id=1, source_target_pairs={{0,2},{2,4},{4,6},{6,8},{8,10},{10,12},{12,14},{14,16},{16,18},{18... | collective-permute-start | bytes 104 | tf_op jit(solution)/shard_map/ppermute | solution.py:36
  197.2 11.5 %collective-permute-start.26 = (f32[8,16384]{1,0:T(8,128)S(1)}, f32[8,16384]{1,0:T(8,128)S(1)}, u32[]{:S(2)}, u32[]{:S(2)}) collective-permute-start(f32[8,16384]{1,0:T(8,128)S(1)} %fusion.44), channel_id=1, source_target_pairs={{0,1},{1,0},{2,3},{3,2},{4,5},{5,4},{6,7},{7,6},{8,9},{9,8},{10,11... | collective-permute-start | bytes 1572872 | tf_op jit(solution)/shard_map/ppermute | solution.py:26
  200.0 8.0 %collective-permute-start.25 = (f32[8,1]{1,0:T(8,128)S(1)}, f32[8,1]{1,0:T(8,128)S(1)}, u32[]{:S(2)}, u32[]{:S(2)}) collective-permute-start(f32[8,1]{1,0:T(8,128)S(1)} %get-tuple-element.12), channel_id=1, source_target_pairs={{2,0},{4,2},{6,4},{8,6},{10,8},{12,10},{14,12},{16,14},{18,16},{20... | collective-permute-start | bytes 104 | tf_op jit(solution)/shard_map/ppermute | solution.py:37
  201.3 7.4 %collective-permute-start.24 = (f32[8,1]{1,0:T(8,128)S(1)}, f32[8,1]{1,0:T(8,128)S(1)}, u32[]{:S(2)}, u32[]{:S(2)}) collective-permute-start(f32[8,1]{1,0:T(8,128)S(1)} %get-tuple-element.11), channel_id=1, source_target_pairs={{0,2},{2,4},{4,6},{6,8},{8,10},{10,12},{12,14},{14,16},{16,18},{18... | collective-permute-start | bytes 104 | tf_op jit(solution)/shard_map/ppermute | solution.py:36
  209.4 13.4 %collective-permute-start.29 = (f32[8,16384]{1,0:T(8,128)S(1)}, f32[8,16384]{1,0:T(8,128)S(1)}, u32[]{:S(2)}, u32[]{:S(2)}) collective-permute-start(f32[8,16384]{1,0:T(8,128)S(1)} %fusion.38), channel_id=1, source_target_pairs={{0,1},{1,0},{2,3},{3,2},{4,5},{5,4},{6,7},{7,6},{8,9},{9,8},{10,11... | collective-permute-start | bytes 1572872 | tf_op jit(solution)/shard_map/ppermute | solution.py:26
  212.2 22.9 %collective-permute-start.33 = (f32[8,16384]{1,0:T(8,128)S(1)}, f32[8,16384]{1,0:T(8,128)S(1)}, u32[]{:S(2)}, u32[]{:S(2)}) collective-permute-start(f32[8,16384]{1,0:T(8,128)S(1)} %fusion.18), channel_id=1, source_target_pairs={{0,1},{1,0},{2,3},{3,2},{4,5},{5,4},{6,7},{7,6},{8,9},{9,8},{10,11... | collective-permute-start | bytes 1572872 | tf_op jit(solution)/shard_map/ppermute | solution.py:26
  214.2 8.5 %collective-permute-start.28 = (f32[8,1]{1,0:T(8,128)S(1)}, f32[8,1]{1,0:T(8,128)S(1)}, u32[]{:S(2)}, u32[]{:S(2)}) collective-permute-start(f32[8,1]{1,0:T(8,128)S(1)} %get-tuple-element.10), channel_id=1, source_target_pairs={{2,0},{4,2},{6,4},{8,6},{10,8},{12,10},{14,12},{16,14},{18,16},{20... | collective-permute-start | bytes 104 | tf_op jit(solution)/shard_map/ppermute | solution.py:37
  223.3 12.0 %collective-permute-start.32 = (f32[8,16384]{1,0:T(8,128)S(1)}, f32[8,16384]{1,0:T(8,128)S(1)}, u32[]{:S(2)}, u32[]{:S(2)}) collective-permute-start(f32[8,16384]{1,0:T(8,128)S(1)} %fusion.32), channel_id=1, source_target_pairs={{0,1},{1,0},{2,3},{3,2},{4,5},{5,4},{6,7},{7,6},{8,9},{9,8},{10,11... | collective-permute-start | bytes 1572872 | tf_op jit(solution)/shard_map/ppermute | solution.py:26
  226.6 8.5 %collective-permute-start.31 = (f32[8,1]{1,0:T(8,128)S(1)}, f32[8,1]{1,0:T(8,128)S(1)}, u32[]{:S(2)}, u32[]{:S(2)}) collective-permute-start(f32[8,1]{1,0:T(8,128)S(1)} %get-tuple-element.8), channel_id=1, source_target_pairs={{2,0},{4,2},{6,4},{8,6},{10,8},{12,10},{14,12},{16,14},{18,16},{20... | collective-permute-start | bytes 104 | tf_op jit(solution)/shard_map/ppermute | solution.py:37
  227.9 7.4 %collective-permute-start.30 = (f32[8,1]{1,0:T(8,128)S(1)}, f32[8,1]{1,0:T(8,128)S(1)}, u32[]{:S(2)}, u32[]{:S(2)}) collective-permute-start(f32[8,1]{1,0:T(8,128)S(1)} %get-tuple-element.7), channel_id=1, source_target_pairs={{0,2},{2,4},{4,6},{6,8},{8,10},{10,12},{12,14},{14,16},{16,18},{18... | collective-permute-start | bytes 104 | tf_op jit(solution)/shard_map/ppermute | solution.py:36
  (16 other events, 468.2 us)
Sparse Core Ops, SparseCore 0:
  10.5 83.2 all-gather.1
  237.9 237.1 reduce-scatter.1
